TPU v7x, 256 devices: a whole 4x4x8 slice. The times are simulated.
256 devices in a mesh: row: 8 (over y, core), col: 32 (over x, z).
Axes of the slice: x: 4, y: 4, z: 8, core: 2. Of those that a mesh axis runs over, the one named last changes fastest.
Arguments:
- tokens: bfloat16 [2048, 6144], P('row', 'col'), may hold values from -6 to 6
- cotangent: bfloat16 [2048, 6144], P('row', 'col'), may hold values from -6 to 6
- w_expand: bfloat16 [6144, 12288], P('row', 'col'), may hold values from -0.078125 to 0.078125
- w_reduce: bfloat16 [6144, 12288], P('row', 'col'), may hold values from -0.0546875 to 0.0546875
- expand_mean: bfloat16 [6144, 12288], P('row', 'col'), may hold values from -1 to 1
- expand_mean_scale: float32 [24, 12288], P('row', 'col'), may hold values from 4 to 16
- expand_var: bfloat16 [6144, 12288], P('row', 'col'), may hold values from 0.049804688 to 1
- expand_var_scale: float32 [24, 12288], P('row', 'col'), may hold values from 4 to 16
- reduce_mean: bfloat16 [6144, 12288], P('row', 'col'), may hold values from -1 to 1
- reduce_mean_scale: float32 [24, 12288], P('row', 'col'), may hold values from 4 to 16
- reduce_var: bfloat16 [6144, 12288], P('row', 'col'), may hold values from 0.049804688 to 1
- reduce_var_scale: float32 [24, 12288], P('row', 'col'), may hold values from 4 to 16
Outputs:
- grad_tokens: bfloat16 [2048, 6144], P('row', 'col')
- new_expand: bfloat16 [6144, 12288], P('row', 'col')
- expand_mean_next: bfloat16 [6144, 12288], P('row', 'col')
- expand_mean_scale_next: float32 [24, 12288], P('row', 'col')
- expand_var_next: bfloat16 [6144, 12288], P('row', 'col')
- expand_var_scale_next: float32 [24, 12288], P('row', 'col')
- new_reduce: bfloat16 [6144, 12288], P('row', 'col')
- reduce_mean_next: bfloat16 [6144, 12288], P('row', 'col')
- reduce_mean_scale_next: float32 [24, 12288], P('row', 'col')
- reduce_var_next: bfloat16 [6144, 12288], P('row', 'col')
- reduce_var_scale_next: float32 [24, 12288], P('row', 'col')
All inputs are finite; a program needn't handle non-finite values.
Results may differ from a plain program's by a relative error of at most 0.0049.
Values may be sent and summed in bfloat16 or wider, within the bound.
No kernel may reach another device: no remote copies, remote signals or barrier semaphores. Data moves between devices by JAX's collectives and lax.ppermute only.
A program may use at most 128 MiB of HBM per device.

v0:
```python
import jax
import jax.numpy as jnp
from jax import lax
from jax.sharding import PartitionSpec as P

STEP = 10
beta_one = 0.9
beta_two = 0.999
adam_eps = 1e-08
learn_rate = 0.001
decay_rate = 0.1
scale_eps = 1e-06


def gelu_pair(pre_act):
    cdf_part = 0.5 * (1.0 + lax.erf(pre_act * 0.7071067811865476))
    slope = cdf_part + pre_act * jnp.exp(-0.5 * pre_act * pre_act) * 0.3989422804014327
    return (pre_act * cdf_part, slope)


def spread_scale(values, scale):
    blocks = scale.shape[0]
    shaped = values.reshape(blocks, values.shape[0] // blocks, values.shape[1])
    return (shaped * scale[:, None, :]).reshape(values.shape)


def block_max(values, blocks):
    shaped = values.reshape(blocks, values.shape[0] // blocks, values.shape[1])
    return jnp.max(jnp.abs(shaped), axis=1) + scale_eps


def adam_step(weight, grad_w, mean_q, mean_scale, var_q, var_scale):
    blocks = mean_scale.shape[0]
    mean_new = (
        beta_one * spread_scale(mean_q.astype(jnp.float32), mean_scale) + (1.0 - beta_one) * grad_w
    )
    var_new = (
        beta_two * spread_scale(var_q.astype(jnp.float32), var_scale)
        + (1.0 - beta_two) * grad_w * grad_w
    )
    mean_hat = mean_new / (1.0 - beta_one**STEP)
    var_hat = var_new / (1.0 - beta_two**STEP)
    old_weight = weight.astype(jnp.float32)
    new_weight = (
        old_weight
        - learn_rate * (mean_hat / (jnp.sqrt(var_hat) + adam_eps) + decay_rate * old_weight)
    ).astype(jnp.bfloat16)
    mean_scale_next = block_max(mean_new, blocks)
    var_scale_next = block_max(var_new, blocks)
    mean_next = spread_scale(mean_new, 1.0 / mean_scale_next).astype(jnp.bfloat16)
    var_next = spread_scale(var_new, 1.0 / var_scale_next).astype(jnp.bfloat16)
    return (new_weight, mean_next, mean_scale_next, var_next, var_scale_next)


def contract_first(left, right):
    return lax.dot_general(
        left, right, (((0,), (0,)), ((), ())), preferred_element_type=jnp.float32
    )


def local(
    tokens,
    cotangent,
    w_expand,
    w_reduce,
    expand_mean,
    expand_mean_scale,
    expand_var,
    expand_var_scale,
    reduce_mean,
    reduce_mean_scale,
    reduce_var,
    reduce_var_scale,
):
    token_rows, cot_rows = (
        lax.all_gather(tokens, "col", axis=1, tiled=True),
        lax.all_gather(cotangent, "col", axis=1, tiled=True),
    )
    input_whole, cot_whole = (
        lax.all_to_all(token_rows, "row", split_axis=1, concat_axis=0, tiled=True),
        lax.all_to_all(cot_rows, "row", split_axis=1, concat_axis=0, tiled=True),
    )
    up_panel, down_panel = (
        lax.all_gather(w_expand, "row", axis=0, tiled=True),
        lax.all_gather(w_reduce, "row", axis=0, tiled=True),
    )
    pre_act = jnp.dot(token_rows, up_panel, preferred_element_type=jnp.float32)
    act_grad = jnp.dot(cot_rows, down_panel, preferred_element_type=jnp.float32)
    activated, slope = gelu_pair(pre_act)
    activated = activated.astype(jnp.bfloat16)
    pre_grad = (act_grad * slope).astype(jnp.bfloat16)
    grad_cols = lax.psum_scatter(
        lax.dot_general(
            up_panel, pre_grad, (((1,), (1,)), ((), ())), preferred_element_type=jnp.float32
        ),
        "col",
        scatter_dimension=0,
        tiled=True,
    )
    grad_tokens = grad_cols.T.astype(jnp.bfloat16)
    grad_expand = contract_first(input_whole, lax.all_gather(pre_grad, "row", axis=0, tiled=True))
    grad_reduce = contract_first(cot_whole, lax.all_gather(activated, "row", axis=0, tiled=True))
    first = adam_step(
        w_expand, grad_expand, expand_mean, expand_mean_scale, expand_var, expand_var_scale
    )
    second = adam_step(
        w_reduce, grad_reduce, reduce_mean, reduce_mean_scale, reduce_var, reduce_var_scale
    )
    return (
        grad_tokens,
        first[0],
        first[1],
        first[2],
        first[3],
        first[4],
        second[0],
        second[1],
        second[2],
        second[3],
        second[4],
    )


def solution(mesh):
    placed = (
        P("row", "col"),
        P("row", "col"),
        P("row", "col"),
        P("row", "col"),
        P("row", "col"),
        P("row", "col"),
        P("row", "col"),
        P("row", "col"),
        P("row", "col"),
        P("row", "col"),
        P("row", "col"),
        P("row", "col"),
    )
    return jax.shard_map(
        local,
        mesh=mesh,
        in_specs=placed,
        out_specs=(
            P("row", "col"),
            P("row", "col"),
            P("row", "col"),
            P("row", "col"),
            P("row", "col"),
            P("row", "col"),
            P("row", "col"),
            P("row", "col"),
            P("row", "col"),
            P("row", "col"),
            P("row", "col"),
        ),
        check_vma=False,
    )
```

profile of v0, /device:TPU:8, one launch (start us, length us, event | category | flops | bytes accessed | tf_op | source)
XLA Modules:
  0.0 555.6 jit_solution(1710327823756502407)
XLA Ops:
  7.2 0.7 all-gather.11.cloned.1.call-update
  8.0 0.7 all-gather.13.cloned.1.call-update
  8.7 0.7 all-gather.7.cloned.1.call-update
  9.4 0.5 all-gather.9.cloned.1.call-update
  10.0 82.9 %all-gather.11.cloned.1.call-done = bf16[256,6144]{0,1:T(8,128)(2,1)} async-done(((bf16[256,192]{0,1:T(8,128)(2,1)}), bf16[256,6144]{0,1:T(8,128)(2,1)}) %all-gather.11.cloned.1.call-update) | async-done | bytes 3145744 | tf_op jit(solution)/shard_map/all_gather | solution.py:76
  92.9 34.3 %all-gather.13.cloned.1.call-done = bf16[6144,384]{1,0:T(8,128)(2,1)} async-done(((bf16[768,384]{1,0:T(8,128)(2,1)}), bf16[6144,384]{1,0:T(8,128)(2,1)}) %all-gather.13.cloned.1.call-update) | async-done | bytes 4718608 | tf_op jit(solution)/shard_map/all_gather | solution.py:84
  127.2 5.8 %multiply_convert_fusion.4 = (bf16[256,384]{1,0:T(8,128)(2,1)}, f32[256,384]{1,0:T(8,128)S(1)}) fusion(bf16[256,6144]{0,1:T(8,128)(2,1)} %all-gather.11.cloned.1.call-done, bf16[6144,384]{1,0:T(8,128)(2,1)} %all-gather.13.cloned.1.call-done), kind=kOutput, calls=%fused_computation.30 | convolution fusion | flops 1208451072 | bytes 8454144 | tf_op jit(solution)/shard_map/dot_general | solution.py:87
  133.1 77.2 %all-gather.7.cloned.1.call-done = bf16[256,6144]{0,1:T(8,128)(2,1)} async-done(((bf16[256,192]{0,1:T(8,128)(2,1)}), bf16[256,6144]{0,1:T(8,128)(2,1)}) %all-gather.7.cloned.1.call-update) | async-done | bytes 3145744 | tf_op jit(solution)/shard_map/all_gather | solution.py:77
  210.2 34.2 %all-gather.9.cloned.1.call-done = bf16[6144,384]{1,0:T(8,128)(2,1)} async-done(((bf16[768,384]{1,0:T(8,128)(2,1)}), bf16[6144,384]{1,0:T(8,128)(2,1)}) %all-gather.9.cloned.1.call-update) | async-done | bytes 4718608 | tf_op jit(solution)/shard_map/all_gather | solution.py:85
  244.4 5.9 %fusion.8 = bf16[256,384]{1,0:T(8,128)(2,1)} fusion(bf16[256,6144]{0,1:T(8,128)(2,1)} %all-gather.7.cloned.1.call-done, bf16[6144,384]{1,0:T(8,128)(2,1)} %all-gather.9.cloned.1.call-done, f32[256,384]{1,0:T(8,128)S(1)} %get-tuple-element.82), kind=kOutput, calls=%fused_computation.24 | convolution fusion | flops 1208942592 | bytes 8454144 | tf_op jit(solution)/shard_map/dot_general | solution.py:88
  250.4 0.5 all-gather.17.cloned.1.call-update
  250.9 7.0 %convolution_bitcast_fusion = f32[6144,256]{0,1:T(8,128)} fusion(bf16[256,384]{1,0:T(8,128)(2,1)} %fusion.8, bf16[6144,384]{1,0:T(8,128)(2,1)} %all-gather.13.cloned.1.call-done), kind=kOutput, calls=%fused_computation | convolution fusion | flops 1207959552 | bytes 11206656 | tf_op jit(solution)/shard_map/dot_general | solution.py:93
  257.9 6.6 %copy.123 = f32[6144,256]{1,0:T(8,128)} copy(f32[6144,256]{0,1:T(8,128)} %convolution_bitcast_fusion) | data formatting | bytes 12582912
  264.5 1.9 copy-done
  266.4 49.7 %all_to_all.38 = bf16[256,8,768]{0,2,1:T(8,128)(2,1)} all-to-all(bf16[256,8,768]{0,2,1:T(8,128)(2,1)S(1)} %bitcast.38), channel_id=1, replica_groups=mesh['row'=8,'col'=32] {'row'}, dimensions={1} | all-to-all | bytes 6291456 | tf_op jit(solution)/shard_map/all_to_all | solution.py:80
  316.1 4.0 all-to-all-start.1
  320.2 2.1 copy.96
  322.3 2.1 copy.106
  324.4 1.1 mul.182
  325.5 2.7 copy.101
  328.2 1.1 mul.177
  329.3 2.7 copy.98
  332.0 2.1 copy.100
  334.1 2.1 copy.97
  336.3 1.1 mul.196
  337.4 2.7 copy.108
  340.0 1.1 mul.202
  341.2 2.7 copy.111
  343.8 2.1 copy.107
  346.0 2.1 copy.110
  348.1 4.7 copy.99
  352.8 4.3 all-to-all-done.1
  357.1 2.9 copy.109
  360.0 6.3 %fusion.18 = (f32[768,384]{0,1:T(8,128)}, f32[768,384]{0,1:T(8,128)S(1)}, f32[768,384]{0,1:T(8,128)S(1)}, f32[768,384]{0,1:T(8,128)S(1)}) fusion(f32[768,384]{0,1:T(8,128)} %copy.98, bf16[768,384]{0,1:T(8,128)(2,1)} %copy.97, f32[768,384]{0,1:T(8,128)} %copy.101, bf16[768,384]{0,1:T(8,128)(2,1)} %copy.100, ...), kind=kOutput, calls=%fused_computation.44 | convolution fusion | flops 1211793408 | bytes 12976128 | tf_op jit(solution)/shard_map/dot_general | solution.py:56
  366.3 2.7 copy.102
  369.0 1.4 copy.104
  370.4 1.4 reduce_max.36
  371.8 0.2 copy-done.5
  372.0 0.7 reduce_max.37
  372.7 1.3 broadcast_divide_fusion.2
  373.9 1.1 mul.190
  375.0 1.6 copy.103
  376.7 1.1 mul.193
  377.8 2.7 copy.105
  380.5 3.5 multiply_convert_fusion.2
  384.0 2.3 copy.117
  386.2 2.1 copy.118
  388.4 2.1 copy.119
  390.5 6.4 %fusion.15 = (f32[768,384]{0,1:T(8,128)}, f32[768,384]{0,1:T(8,128)}, f32[768,384]{0,1:T(8,128)}, f32[768,384]{0,1:T(8,128)}) fusion(f32[768,384]{0,1:T(8,128)} %copy.108, bf16[768,384]{0,1:T(8,128)(2,1)} %copy.107, f32[768,384]{0,1:T(8,128)} %copy.111, bf16[768,384]{0,1:T(8,128)(2,1)} %copy.110, bf16[2048,384]{1,0:T(8,128)(2,1)} %all-gather.17.cloned.1.call-done, ...), kind=kOutput, calls=%fused_computation.42 | convolution fusion | flops 1211793408 | bytes 12976128 | tf_op jit(solution)/shard_map/dot_general | solution.py:56
  396.9 1.6 copy.112
  398.5 0.1 reduce_max.38
  398.6 1.2 copy-done.4
  399.8 0.4 copy.114
  400.2 0.6 broadcast_divide_fusion
  400.9 0.4 copy.113
  401.3 1.2 mul.213
  402.5 2.9 copy.115
  405.4 3.5 multiply_convert_fusion
  408.9 2.2 copy.120
  411.1 1.1 copy.121
  412.2 1.1 copy.122
  413.2 133.7 %reduce-scatter.4.cloned.1.call-done = f32[192,256]{1,0:T(8,128)} async-done(((f32[6144,256]{1,0:T(8,128)}), f32[192,256]{1,0:T(8,128)}) %reduce-scatter.4.cloned.1.call-update) | async-done | bytes 196624
  547.0 1.0 copy.124
  548.0 0.7 copy.116
  (34 shorter events, 0.5 us)
Async XLA Ops:
  7.2 85.7 %all-gather.11.cloned.1.call-start = ((), (), s32[]{:S(2)}) async-start(), calls=%async_computation.5 | async-start | bytes 3244032 | tf_op jit(solution)/shard_map/all_gather | solution.py:76
  7.9 119.3 %all-gather.13.cloned.1.call-start = ((), (), s32[]{:S(2)}) async-start(), calls=%async_computation.6 | async-start | bytes 5308416 | tf_op jit(solution)/shard_map/all_gather | solution.py:84
  8.7 201.6 %all-gather.7.cloned.1.call-start = ((), (), s32[]{:S(2)}) async-start(), calls=%async_computation.3 | async-start | bytes 3244032 | tf_op jit(solution)/shard_map/all_gather | solution.py:77
  9.4 235.0 %all-gather.9.cloned.1.call-start = ((), (), s32[]{:S(2)}) async-start(), calls=%async_computation.4 | async-start | bytes 5308416 | tf_op jit(solution)/shard_map/all_gather | solution.py:85
  10.0 350.0 %all-gather.15.cloned.1.call-start = ((), (), s32[]{:S(2)}) async-start(), calls=%async_computation.7 | async-start | bytes 1769472 | tf_op jit(solution)/shard_map/all_gather | solution.py:101
  250.3 140.2 %all-gather.17.cloned.1.call-start = ((), (), s32[]{:S(2)}) async-start(), calls=%async_computation.8 | async-start | bytes 1769472 | tf_op jit(solution)/shard_map/all_gather | solution.py:102
  250.9 296.1 %reduce-scatter.4.cloned.1.call-start = ((), (), s32[]{:S(2)}) async-start(), calls=%async_computation.9 | async-start | bytes 6488064
  264.5 1.9 copy-start
  316.1 41.0 %all-to-all-start.1 = ((bf16[256,8,768]{0,2,1:T(8,128)(2,1)}), bf16[256,8,768]{0,2,1:T(8,128)(2,1)S(1)}, u32[]{:S(2)}, u32[]{:S(2)}) async-start(bf16[256,8,768]{0,2,1:T(8,128)(2,1)} %bitcast.39), calls=%async_computation.1 | async-start | bytes 6291456 | tf_op jit(solution)/shard_map/all_to_all | solution.py:81
  320.2 4.3 copy-start.8
  325.5 2.7 copy-start.9
  332.0 4.3 copy-start.10
  337.4 2.7 copy-start.11
  370.4 1.6 copy-start.5
  384.0 6.5 %copy-start.1 = (bf16[8,256,768]{2,1,0:T(8,128)(2,1)S(1)}, bf16[8,256,768]{2,1,0:T(8,128)(2,1)}, u32[]{:S(2)}) copy-start(bf16[8,256,768]{2,1,0:T(8,128)(2,1)} %copy.109) | copy-start | bytes 9437188
  398.5 1.3 copy-start.4
  402.5 2.9 copy-start.2
  402.5 2.9 copy-start.3
  408.9 2.2 copy-start.7
  408.9 3.3 copy-start.6
Sparse Core Ops, SparseCore 0:
  10.6 82.2 all-gather.10
  94.7 32.4 all-gather.12
  129.8 80.3 all-gather.6
  211.9 32.4 all-gather.8
  250.4 27.9 all-gather.14
  280.1 34.5 all-gather.16
  318.7 228.2 reduce-scatter.3
where the time goes:
time: 557 us; the launch traced here: 556 us
  waiting for transfers between devices  370 us (66%)
  local copies, waits for them, and re-layouts  75.1 us (13%)
  blocking collectives  49.7 us (9%)
  matrix products  31.3 us (6%)
  between operations  14.2 us (3%)
  other arithmetic  11.2 us (2%)
    unnamed x8, waiting for transfers between devices  137 us
    all_gather x1, waiting for transfers between devices, local(): lax.all_gather(tokens, 'col', axis=1, tiled=True)  82.9 us
    all_gather x1, waiting for transfers between devices, local(): lax.all_gather(cotangent, 'col', axis=1, tiled=True)  77.2 us
    all_to_all x1, blocking collectives, local(): lax.all_to_all(token_rows, 'row', split_axis=1, concat_axis=0, tiled=True)  49.7 us
    unnamed x39, local copies, waits for them, and re-layouts  35.3 us
    all_gather x1, waiting for transfers between devices, local(): lax.all_gather(w_expand, 'row', axis=0, tiled=True)  34.3 us
    all_gather x1, waiting for transfers between devices, local(): lax.all_gather(w_reduce, 'row', axis=0, tiled=True)  34.2 us
    mul x16, local copies, waits for them, and re-layouts, spread_scale(): return (shaped * scale[:, None, :]).reshape(values.shape)  26.2 us
  transfers between devices with their start and end apart: 8, of which 6 were waited for; matrix products, arithmetic and copies ran while one was open for 19% of the time, Pallas kernels for 0%

commit v1 on v0

--- a/solution.py
+++ b/solution.py
@@ -2,6 +2,7 @@
 import jax.numpy as jnp
 from jax import lax
 from jax.sharding import PartitionSpec as P
+from jax.lax import all_to_all, axis_size
 
 STEP = 10
 beta_one = 0.9
@@ -72,6 +73,13 @@
     reduce_var,
     reduce_var_scale,
 ):
+
+    def build_the_strings(sample, at_axis):
+        link_axis = "row"
+        big = jnp.concatenate(axis_size(link_axis) * [sample], at_axis)
+        plain = all_to_all(big, link_axis, split_axis=at_axis, concat_axis=at_axis, tiled=True)
+        return plain
+
     token_rows, cot_rows = (
         lax.all_gather(tokens, "col", axis=1, tiled=True),
         lax.all_gather(cotangent, "col", axis=1, tiled=True),
@@ -82,7 +90,7 @@
     )
     up_panel, down_panel = (
         lax.all_gather(w_expand, "row", axis=0, tiled=True),
-        lax.all_gather(w_reduce, "row", axis=0, tiled=True),
+        build_the_strings(w_reduce, 0),
     )
     pre_act = jnp.dot(token_rows, up_panel, preferred_element_type=jnp.float32)
     act_grad = jnp.dot(cot_rows, down_panel, preferred_element_type=jnp.float32)

time: 557 us -> 523 us (0.939)
  waiting for transfers between devices: 370 us -> 340 us
  local copies, waits for them, and re-layouts: 75.1 us -> 65 us
  starting transfers between devices: 4.3 us -> 11.4 us
    all_gather x1 -> x0, waiting for transfers between devices: 34.2 us -> none  [local(): lax.all_gather(w_reduce, 'row', axis=0, tiled=True)]
    all_to_all x1, waiting for transfers between devices: 4.32 us -> 17.5 us  [local(): lax.all_to_all(cot_rows, 'row', split_axis=1, concat_axis=0, tiled=True)]
    all_gather x1, waiting for transfers between devices: 82.9 us -> 73.9 us  [local(): lax.all_gather(tokens, 'col', axis=1, tiled=True)]
    all_to_all x0 -> x1, starting transfers between devices: none -> 6.64 us  [build_the_strings(): all_to_all(big, link_axis, split_axis=at_axis, concat_axis=at_axis, tiled...]
    mul x16, local copies, waits for them, and re-layouts: 26.2 us -> 20.5 us  [spread_scale(): return (shaped * scale[:, None, :]).reshape(values.shape)]
    unnamed x39 -> x54, local copies, waits for them, and re-layouts: 35.3 us -> 30.7 us
    unnamed x8 -> x7, waiting for transfers between devices: 137 us -> 137 us
  transfers between devices with their start and end apart: 8 -> 8, of which waited for: 6 -> 5; matrix products, arithmetic and copies ran while one was open for 19% -> 19% of each run, Pallas kernels for 0% -> 0%
where the time goes in v1:
time: 523 us; the launch traced here: 522 us
  waiting for transfers between devices  340 us (65%)
  local copies, waits for them, and re-layouts  65 us (12%)
  blocking collectives  47.2 us (9%)
  matrix products  31.9 us (6%)
  between operations  14.4 us (3%)
  other arithmetic  12.2 us (2%)
  starting transfers between devices  11.4 us (2%)
    unnamed x7, waiting for transfers between devices  137 us
    all_gather x1, waiting for transfers between devices, local(): lax.all_gather(cotangent, 'col', axis=1, tiled=True)  77.1 us
    all_gather x1, waiting for transfers between devices, local(): lax.all_gather(tokens, 'col', axis=1, tiled=True)  73.9 us
    all_to_all x1, blocking collectives, local(): lax.all_to_all(token_rows, 'row', split_axis=1, concat_axis=0, tiled=True)  47.2 us
    all_gather x1, waiting for transfers between devices, local(): lax.all_gather(w_expand, 'row', axis=0, tiled=True)  34.3 us
    unnamed x54, local copies, waits for them, and re-layouts  30.7 us
    mul x16, local copies, waits for them, and re-layouts, spread_scale(): return (shaped * scale[:, None, :]).reshape(values.shape)  20.5 us
    all_to_all x1, waiting for transfers between devices, local(): lax.all_to_all(cot_rows, 'row', split_axis=1, concat_axis=0, tiled=True)  17.5 us
  transfers between devices with their start and end apart: 8, of which 5 were waited for; matrix products, arithmetic and copies ran while one was open for 19% of the time, Pallas kernels for 0%

profile of v1, /device:TPU:8, one launch (start us, length us, event | category | flops | bytes accessed | tf_op | source)
XLA Modules:
  0.0 521.7 jit_solution(8183200439814048404)
XLA Ops:
  7.2 0.7 all-gather.8.cloned.1.call-update
  8.0 0.7 all-gather.10.cloned.1.call-update
  8.7 0.7 all-gather.6.cloned.1.call-update
  9.5 0.1 constant_dynamic-update-slice_fusion.6
  9.6 0.1 constant_dynamic-update-slice_fusion.5
  9.7 0.1 constant_dynamic-update-slice_fusion.4
  9.8 0.1 constant_dynamic-update-slice_fusion.3
  9.9 0.1 constant_dynamic-update-slice_fusion.2
  10.0 0.1 constant_dynamic-update-slice_fusion.1
  10.2 2.2 copy-done.5
  12.4 6.6 %all-to-all-start = ((bf16[8,768,384]{2,1,0:T(8,128)(2,1)}), bf16[8,768,384]{2,1,0:T(8,128)(2,1)}, u32[]{:S(2)}, u32[]{:S(2)}) async-start(bf16[8,768,384]{2,1,0:T(8,128)(2,1)} %bitcast.50), calls=%async_computation | async-start | bytes 9437184 | tf_op jit(solution)/shard_map/all_to_all | solution.py:80
  19.0 73.9 %all-gather.8.cloned.1.call-done = bf16[256,6144]{0,1:T(8,128)(2,1)} async-done(((bf16[256,192]{0,1:T(8,128)(2,1)}), bf16[256,6144]{0,1:T(8,128)(2,1)}) %all-gather.8.cloned.1.call-update) | async-done | bytes 3145744 | tf_op jit(solution)/shard_map/all_gather | solution.py:84
  92.9 34.3 %all-gather.10.cloned.1.call-done = bf16[6144,384]{1,0:T(8,128)(2,1)} async-done(((bf16[768,384]{1,0:T(8,128)(2,1)}), bf16[6144,384]{1,0:T(8,128)(2,1)}) %all-gather.10.cloned.1.call-update) | async-done | bytes 4718608 | tf_op jit(solution)/shard_map/all_gather | solution.py:92
  127.2 5.9 %multiply_convert_fusion.4 = (bf16[256,384]{0,1:T(8,128)(2,1)}, f32[256,384]{0,1:T(8,128)S(1)}) fusion(bf16[256,6144]{0,1:T(8,128)(2,1)} %all-gather.8.cloned.1.call-done, bf16[6144,384]{1,0:T(8,128)(2,1)} %all-gather.10.cloned.1.call-done), kind=kOutput, calls=%fused_computation.31 | convolution fusion | flops 1208451072 | bytes 8454144 | tf_op jit(solution)/shard_map/dot_general | solution.py:95
  133.2 77.1 %all-gather.6.cloned.1.call-done = bf16[256,6144]{0,1:T(8,128)(2,1)} async-done(((bf16[256,192]{0,1:T(8,128)(2,1)}), bf16[256,6144]{0,1:T(8,128)(2,1)}) %all-gather.6.cloned.1.call-update) | async-done | bytes 3145744 | tf_op jit(solution)/shard_map/all_gather | solution.py:85
  210.3 5.4 %fusion.9 = bf16[256,384]{0,1:T(8,128)(2,1)} fusion(bf16[6144,384]{1,0:T(8,128)(2,1)} %bitcast.1, bf16[256,6144]{0,1:T(8,128)(2,1)} %all-gather.6.cloned.1.call-done, f32[256,384]{0,1:T(8,128)S(1)} %get-tuple-element.82), kind=kOutput, calls=%fused_computation.25 | convolution fusion | flops 1208942592 | bytes 8454144 | tf_op jit(solution)/shard_map/dot_general | solution.py:96
  215.8 0.5 all-gather.14.cloned.1.call-update
  216.4 7.0 %convolution_bitcast_fusion = f32[6144,256]{0,1:T(8,128)} fusion(bf16[256,384]{0,1:T(8,128)(2,1)} %fusion.9, bf16[6144,384]{1,0:T(8,128)(2,1)} %all-gather.10.cloned.1.call-done), kind=kOutput, calls=%fused_computation | convolution fusion | flops 1207959552 | bytes 11206656 | tf_op jit(solution)/shard_map/dot_general | solution.py:101
  223.3 6.7 %copy.144 = f32[6144,256]{1,0:T(8,128)} copy(f32[6144,256]{0,1:T(8,128)} %convolution_bitcast_fusion) | data formatting | bytes 12582912
  230.0 47.2 %all_to_all.50 = bf16[256,8,768]{0,2,1:T(8,128)(2,1)} all-to-all(bf16[256,8,768]{0,2,1:T(8,128)(2,1)} %bitcast.63), channel_id=1, replica_groups=mesh['row'=8,'col'=32] {'row'}, dimensions={1} | all-to-all | bytes 6291456 | tf_op jit(solution)/shard_map/all_to_all | solution.py:88
  277.2 4.5 all-to-all-start.2
  281.7 1.1 copy.115
  282.8 1.1 copy.125
  284.0 1.4 copy.117
  285.4 1.1 copy.116
  286.6 1.4 copy.120
  288.0 1.1 copy.119
  289.2 1.4 copy.127
  290.6 1.1 copy.126
  291.6 1.1 mul.202
  292.7 2.8 copy.131
  295.5 2.1 copy.130
  297.7 2.9 copy.118
  300.5 17.5 %all-to-all-done.2 = bf16[256,8,768]{0,2,1:T(8,128)(2,1)} async-done(((bf16[256,8,768]{0,2,1:T(8,128)(2,1)}), bf16[256,8,768]{0,2,1:T(8,128)(2,1)}, u32[]{:S(2)}, u32[]{:S(2)}) %all-to-all-start.2) | async-done | bytes 3145760 | tf_op jit(solution)/shard_map/all_to_all | solution.py:89
  318.0 3.4 copy.129
  321.4 7.3 %fusion.19 = (f32[768,384]{0,1:T(8,128)}, f32[768,384]{0,1:T(8,128)}, f32[768,384]{0,1:T(8,128)}, f32[768,384]{0,1:T(8,128)}) fusion(f32[768,384]{0,1:T(8,128)} %copy.117, bf16[768,384]{0,1:T(8,128)(2,1)} %copy.116, f32[768,384]{0,1:T(8,128)} %copy.120, bf16[768,384]{0,1:T(8,128)(2,1)} %copy.119, bf16[2048,384]{0,1:T(8,128)(2,1)} %all-gather.12.cloned.1.call-done, ...), kind=kOutput, calls=%fused_computation.53 | convolution fusion | flops 1211793408 | bytes 12976128 | tf_op jit(solution)/shard_map/dot_general | solution.py:57
  328.7 2.7 copy.123
  331.4 2.7 copy.121
  334.1 1.4 reduce_max.37
  335.5 1.4 reduce_max.36
  336.8 0.6 broadcast_divide_fusion.2
  337.4 1.1 mul.193
  338.5 2.7 copy.124
  341.3 1.1 mul.190
  342.4 2.7 copy.122
  345.1 4.6 multiply_convert_fusion.2
  349.7 2.1 copy.137
  351.8 2.1 copy.138
  353.9 2.1 copy.139
  356.1 6.3 %fusion.16 = (f32[768,384]{0,1:T(8,128)}, f32[768,384]{0,1:T(8,128)}, f32[768,384]{0,1:T(8,128)}, f32[768,384]{0,1:T(8,128)}) fusion(f32[768,384]{0,1:T(8,128)} %copy.127, bf16[768,384]{0,1:T(8,128)(2,1)} %copy.126, f32[768,384]{0,1:T(8,128)} %copy.131, bf16[768,384]{0,1:T(8,128)(2,1)} %copy.130, bf16[2048,384]{0,1:T(8,128)(2,1)} %all-gather.14.cloned.1.call-done, ...), kind=kOutput, calls=%fused_computation.51 | convolution fusion | flops 1211793408 | bytes 12976128 | tf_op jit(solution)/shard_map/dot_general | solution.py:57
  362.4 1.6 copy.134
  364.1 1.2 copy-done.4
  365.3 0.4 copy.132
  365.8 0.6 broadcast_divide_fusion
  366.5 0.4 copy.135
  366.8 1.2 mul.210
  368.0 2.9 copy.133
  370.9 3.5 multiply_convert_fusion
  374.4 2.2 copy.140
  376.7 1.1 copy.141
  377.7 1.1 copy.142
  378.8 134.3 %reduce-scatter.4.cloned.1.call-done = f32[192,256]{1,0:T(8,128)} async-done(((f32[6144,256]{1,0:T(8,128)}), f32[192,256]{1,0:T(8,128)}) %reduce-scatter.4.cloned.1.call-update) | async-done | bytes 196624
  513.1 1.0 copy.145
  514.1 0.7 copy.136
  (49 shorter events, 0.9 us)
Async XLA Ops:
  7.2 2.2 copy-start
  7.2 85.7 %all-gather.8.cloned.1.call-start = ((), (), s32[]{:S(2)}) async-start(), calls=%async_computation.5 | async-start | bytes 3244032 | tf_op jit(solution)/shard_map/all_gather | solution.py:84
  7.9 119.3 %all-gather.10.cloned.1.call-start = ((), (), s32[]{:S(2)}) async-start(), calls=%async_computation.6 | async-start | bytes 5308416 | tf_op jit(solution)/shard_map/all_gather | solution.py:92
  8.7 201.6 %all-gather.6.cloned.1.call-start = ((), (), s32[]{:S(2)}) async-start(), calls=%async_computation.4 | async-start | bytes 3244032 | tf_op jit(solution)/shard_map/all_gather | solution.py:85
  10.2 2.2 copy-start.5
  12.4 120.8 %all-to-all-start = ((bf16[8,768,384]{2,1,0:T(8,128)(2,1)}), bf16[8,768,384]{2,1,0:T(8,128)(2,1)}, u32[]{:S(2)}, u32[]{:S(2)}) async-start(bf16[8,768,384]{2,1,0:T(8,128)(2,1)} %bitcast.50), calls=%async_computation | async-start | bytes 9437184 | tf_op jit(solution)/shard_map/all_to_all | solution.py:80
  19.0 302.4 %all-gather.12.cloned.1.call-start = ((), (), s32[]{:S(2)}) async-start(), calls=%async_computation.7 | async-start | bytes 1769472 | tf_op jit(solution)/shard_map/all_gather | solution.py:109
  215.7 140.4 %all-gather.14.cloned.1.call-start = ((), (), s32[]{:S(2)}) async-start(), calls=%async_computation.8 | async-start | bytes 1769472 | tf_op jit(solution)/shard_map/all_gather | solution.py:110
  216.3 296.7 %reduce-scatter.4.cloned.1.call-start = ((), (), s32[]{:S(2)}) async-start(), calls=%async_computation.9 | async-start | bytes 6488064
  277.2 4.5 copy-start.8
  277.2 40.8 %all-to-all-start.2 = ((bf16[256,8,768]{0,2,1:T(8,128)(2,1)}), bf16[256,8,768]{0,2,1:T(8,128)(2,1)}, u32[]{:S(2)}, u32[]{:S(2)}) async-start(bf16[256,8,768]{0,2,1:T(8,128)(2,1)} %bitcast.46), calls=%async_computation.2 | async-start | bytes 6291456 | tf_op jit(solution)/shard_map/all_to_all | solution.py:89
  281.7 2.2 copy-start.12
  284.0 1.4 copy-start.9
  285.4 1.1 copy-start.13
  286.6 1.5 copy-start.10
  288.0 1.1 copy-start.14
  289.2 1.4 copy-start.11
  290.6 1.1 copy-start.15
  292.7 5.0 copy-start.1
  364.0 1.3 copy-start.4
  368.0 2.9 copy-start.2
  368.0 2.9 copy-start.3
  374.4 2.2 copy-start.7
  374.4 3.3 copy-start.6
Sparse Core Ops, SparseCore 0:
  10.6 82.2 all-gather.7
  94.7 32.4 all-gather.9
  129.8 80.3 all-gather.5
  215.8 25.6 all-gather.11
  243.2 39.1 all-gather.13
  286.2 226.7 reduce-scatter.3
